TPU v7x, 32 devices: a whole 2x2x4 slice. The times are simulated.
32 devices in a mesh: groups: 2 (over x), width: 16 (over z, y, core).
Axes of the slice: x: 2, y: 2, z: 4, core: 2. Of those that a mesh axis runs over, the one named last changes fastest.
Arguments:
- stream_in: bfloat16 [2, 128, 8192], P(None, 'groups', 'width'), parts along dimension 1, may hold values from -16 to 16
- norm_gain: float32 [2, 8192], replicated, may hold values from 0.1 to 1.9
- w_gate: bfloat16 [2, 8192, 14336], P(None, None, 'width'), may hold values from -0.0625 to 0.0625
- w_up: bfloat16 [2, 8192, 14336], P(None, None, 'width'), may hold values from -0.0625 to 0.0625
- w_down: bfloat16 [2, 14336, 8192], P(None, 'width'), may hold values from -0.0625 to 0.0625
Outputs:
- stream_out: bfloat16 [2, 128, 8192], P(None, 'groups', 'width'), parts along dimension 1
There are 2 independent parts, one for each index of `groups`. A program takes and returns all parts, laid end to end along the dimension named above; an argument that names none is the same for every part. Nothing has to cross between parts.
All inputs are finite; a program needn't handle non-finite values.
Results may differ from a plain program's by a relative error of at most 0.012.
Values may be sent and summed in bfloat16 or wider, within the bound.
A program may use at most 192 MiB of HBM per device.

v0:
```python
import jax
import jax.numpy as jnp
from jax import lax
from jax.sharding import PartitionSpec as P

LAYERS = 2
MICRO = 2


def body(stream_in, norm_gain, w_gate, w_up, w_down):
    width_local = stream_in.shape[2]
    offset = lax.axis_index("width") * width_local
    starts = [
        lax.all_gather(stream_in[micro_index], "width", axis=1, tiled=True)
        for micro_index in range(MICRO)
    ]
    results = []
    for micro_index in range(MICRO):
        stream = starts[micro_index]
        for depth in range(LAYERS):
            stream_f = stream.astype(jnp.float32)
            meansq = jnp.mean(stream_f * stream_f, axis=1, keepdims=True)
            normed = (stream_f * lax.rsqrt(meansq + 1e-05) * norm_gain[depth]).astype(jnp.bfloat16)
            gate_out = jnp.dot(normed, w_gate[depth], preferred_element_type=jnp.float32)
            up_out = jnp.dot(normed, w_up[depth], preferred_element_type=jnp.float32)
            hidden = (jax.nn.silu(gate_out) * up_out).astype(jnp.bfloat16)
            partials = jnp.dot(hidden, w_down[depth], preferred_element_type=jnp.float32)
            branch = lax.psum(partials, "width")
            stream = (stream_f + branch).astype(jnp.bfloat16)
        results.append(stream)
    results = [lax.dynamic_slice_in_dim(stream, offset, width_local, 1) for stream in results]
    return jnp.stack(results)


def solution(mesh):
    return jax.shard_map(
        body,
        mesh=mesh,
        in_specs=(
            P(None, "groups", "width"),
            P(),
            P(None, None, "width"),
            P(None, None, "width"),
            P(None, "width", None),
        ),
        out_specs=P(None, "groups", "width"),
        check_vma=False,
    )
```

profile of v0, /device:TPU:0, one launch (start us, length us, event | category | flops | bytes accessed | tf_op | source)
XLA Modules:
  0.0 415.5 jit_solution(16510495588360910265)
XLA Ops:
  6.5 0.0 all-gather.5.cloned.1.call-start
  6.5 1.5 fusion.118
  8.1 0.0 all-gather.5.cloned.1.call-update
  8.1 0.0 all-gather.7.cloned.1.call-start
  8.1 0.7 all-gather.7.cloned.1.call-update
  8.8 0.0 all-reduce.7.cloned.1.call-start
  8.9 1.0 fusion.119
  9.9 39.0 %all-gather.5.cloned.1.call-done = bf16[1,64,8192]{2,1,0:T(8,128)(2,1)} async-done(((bf16[1,64,512]{2,1,0:T(8,128)(2,1)}), bf16[1,64,8192]{2,1,0:T(8,128)(2,1)}) %all-gather.5.cloned.1.call-update) | async-done | bytes 1048592 | tf_op jit(solution)/shard_map/all_gather | solution.py:14
  48.9 0.0 copy-start
  48.9 1.6 fusion.36
  50.5 36.8 %all-gather.7.cloned.1.call-done = bf16[1,64,8192]{2,1,0:T(8,128)(2,1)} async-done(((bf16[1,64,512]{2,1,0:T(8,128)(2,1)}), bf16[1,64,8192]{2,1,0:T(8,128)(2,1)}) %all-gather.7.cloned.1.call-update) | async-done | bytes 1048592 | tf_op jit(solution)/shard_map/all_gather | solution.py:14
  87.3 1.5 fusion.40
  88.9 0.0 copy-done
  88.9 0.0 copy-start.1
  88.9 6.7 %fusion.22 = f32[64,896]{1,0:T(8,128)S(1)} fusion(bf16[2,8192,896]{2,1,0:T(8,128)(2,1)} %param.7, bf16[1,64,8192]{2,1,0:T(8,128)(2,1)S(1)} %copy-done, f32[8192]{0:T(1024)S(1)} %bitcast.82, f32[64]{0:T(128)S(1)} %add_rsqrt_fusion.3), kind=kOutput, calls=%fused_computation.22 | convolution fusion | flops 941621248 | bytes 15991040 | tf_op jit(solution)/shard_map/dot_general | solution.py:24
  95.6 0.0 copy-done.1
  95.6 6.6 %fusion.20 = f32[64,896]{1,0:T(8,128)S(1)} fusion(bf16[2,8192,896]{2,1,0:T(8,128)(2,1)} %param.7, bf16[1,64,8192]{2,1,0:T(8,128)(2,1)S(1)} %copy-done.1, f32[64]{0:T(128)S(1)} %add_rsqrt_fusion.1, f32[8192]{0:T(1024)S(1)} %bitcast.83), kind=kOutput, calls=%fused_computation.20 | convolution fusion | flops 941621248 | bytes 15991040 | tf_op jit(solution)/shard_map/dot_general | solution.py:24
  102.2 16.4 %fusion.14 = f32[64,8192]{1,0:T(8,128)} fusion(bf16[2,896,8192]{2,1,0:T(8,128)(2,1)} %param.9, bf16[2,8192,896]{2,1,0:T(8,128)(2,1)} %param.8, bf16[1,64,8192]{2,1,0:T(8,128)(2,1)S(1)} %copy-done, f32[8192]{0:T(1024)S(1)} %bitcast.84, f32[64]{0:T(128)S(1)} %add_rsqrt_fusion.3, f32[64,896]{1,0:T(8,128)S(1)} %fusion.22), kind=kOutput, calls=%fused_computation.14 | convolution fusion | flops 1881489408 | bytes 32768256 | tf_op jit(solution)/shard_map/dot_general | solution.py:27
  118.6 16.3 %fusion.12 = f32[64,8192]{1,0:T(8,128)} fusion(bf16[2,896,8192]{2,1,0:T(8,128)(2,1)} %param.9, bf16[2,8192,896]{2,1,0:T(8,128)(2,1)} %param.8, bf16[1,64,8192]{2,1,0:T(8,128)(2,1)S(1)} %copy-done.1, f32[64]{0:T(128)S(1)} %add_rsqrt_fusion.1, f32[8192]{0:T(1024)S(1)} %bitcast.85, f32[64,896]{1,0:T(8,128)S(1)} %fusion.20), kind=kOutput, calls=%fused_computation.12 | convolution fusion | flops 1881489408 | bytes 32768256 | tf_op jit(solution)/shard_map/dot_general | solution.py:27
  134.9 0.0 all-reduce.7.cloned.1.call-update
  134.9 0.2 all-reduce.5.cloned.1.call-start
  135.2 110.9 %all-reduce.7.cloned.1.call-done = (f32[64,8192]{1,0:T(8,128)}, f32[64,8192]{1,0:T(8,128)}) async-done(((f32[64,8192]{1,0:T(8,128)}, f32[64,8192]{1,0:T(8,128)}), (f32[64,8192]{1,0:T(8,128)}, f32[64,8192]{1,0:T(8,128)})) %all-reduce.7.cloned.1.call-update) | async-done | bytes 4194320 | tf_op jit(solution)/shard_map/psum | solution.py:28
  246.0 4.2 %multiply_reduce_fusion = (f32[64]{0:T(128)S(1)}, f32[64,8192]{1,0:T(8,128)}, f32[64]{0:T(128)S(1)}, f32[64,8192]{1,0:T(8,128)S(1)}) fusion(f32[64,8192]{1,0:T(8,128)} %get-tuple-element.7, bf16[1,64,8192]{2,1,0:T(8,128)(2,1)S(1)} %copy-done.1, f32[64,8192]{1,0:T(8,128)} %get-tuple-element.8, bf16[1,64,8192]{2,1,0:T(8,128)(2,1)S(1)} %copy-done), kind=kLoop, calls=%fused_computation.51 | loop fusion | flops 6291328 | bytes 10486272 | tf_op jit(solution)/shard_map/reduce_sum | solution.py:22
  250.2 0.0 copy-start.3
  250.2 1.3 copy-done.3
  251.6 6.6 %fusion.10 = f32[64,896]{1,0:T(8,128)S(1)} fusion(bf16[2,8192,896]{2,1,0:T(8,128)(2,1)} %param.7, f32[64,8192]{1,0:T(8,128)S(1)} %get-tuple-element.18, f32[8192]{0:T(1024)S(1)} %bitcast.78, f32[64]{0:T(128)S(1)} %add_rsqrt_fusion.2), kind=kOutput, calls=%fused_computation.10 | convolution fusion | flops 941096960 | bytes 17039616 | tf_op jit(solution)/shard_map/dot_general | solution.py:24
  258.2 0.0 copy-start.2
  258.2 14.6 %fusion.2 = f32[64,8192]{1,0:T(8,128)} fusion(bf16[2,896,8192]{2,1,0:T(8,128)(2,1)} %param.9, bf16[2,8192,896]{2,1,0:T(8,128)(2,1)} %param.8, f32[64,896]{1,0:T(8,128)S(1)} %fusion.10, f32[64,8192]{1,0:T(8,128)} %copy-done.3, f32[8192]{0:T(1024)S(1)} %bitcast.79, f32[64]{0:T(128)S(1)} %add_rsqrt_fusion.2), kind=kOutput, calls=%fused_computation.2 | convolution fusion | flops 1880965120 | bytes 33816832 | tf_op jit(solution)/shard_map/dot_general | solution.py:27
  272.8 0.0 copy-done.2
  272.8 6.6 %fusion.8 = f32[64,896]{1,0:T(8,128)S(1)} fusion(bf16[2,8192,896]{2,1,0:T(8,128)(2,1)} %param.7, f32[64,8192]{1,0:T(8,128)S(1)} %copy-done.2, f32[64]{0:T(128)S(1)} %add_rsqrt_fusion, f32[8192]{0:T(1024)S(1)} %bitcast.80), kind=kOutput, calls=%fused_computation.8 | convolution fusion | flops 941096960 | bytes 17039616 | tf_op jit(solution)/shard_map/dot_general | solution.py:24
  279.5 16.4 %fusion = f32[64,8192]{1,0:T(8,128)} fusion(bf16[2,896,8192]{2,1,0:T(8,128)(2,1)} %param.9, bf16[2,8192,896]{2,1,0:T(8,128)(2,1)} %param.8, f32[64,896]{1,0:T(8,128)S(1)} %fusion.8, f32[64,8192]{1,0:T(8,128)S(1)} %copy-done.2, f32[64]{0:T(128)S(1)} %add_rsqrt_fusion, f32[8192]{0:T(1024)S(1)} %bitcast.81), kind=kOutput, calls=%fused_computation | convolution fusion | flops 1880965120 | bytes 33816832 | tf_op jit(solution)/shard_map/dot_general | solution.py:27
  295.8 0.0 all-reduce.5.cloned.1.call-update
  295.9 110.6 %all-reduce.5.cloned.1.call-done = (f32[64,8192]{1,0:T(8,128)}, f32[64,8192]{1,0:T(8,128)}) async-done(((f32[64,8192]{1,0:T(8,128)}, f32[64,8192]{1,0:T(8,128)}), (f32[64,8192]{1,0:T(8,128)}, f32[64,8192]{1,0:T(8,128)})) %all-reduce.5.cloned.1.call-update) | async-done | bytes 4194320 | tf_op jit(solution)/shard_map/psum | solution.py:28
  406.4 1.0 fusion.110
  407.4 0.9 fusion.111
  408.3 0.7 pad_maximum_fusion
  (4 shorter events, 0.0 us)
Async XLA Ops:
  6.5 42.4 %all-gather.5.cloned.1.call-start = ((), (), s32[]{:S(2)}) async-start(), calls=%async_computation | async-start | bytes 1114112 | tf_op jit(solution)/shard_map/all_gather | solution.py:14
  8.1 79.3 %all-gather.7.cloned.1.call-start = ((), (), s32[]{:S(2)}) async-start(), calls=%async_computation.1 | async-start | bytes 1114112 | tf_op jit(solution)/shard_map/all_gather | solution.py:14
  8.8 237.2 %all-reduce.7.cloned.1.call-start = ((), (), s32[]{:S(2)}) async-start(), calls=%async_computation.3 | async-start | bytes 8388608 | tf_op jit(solution)/shard_map/psum | solution.py:28
  48.9 40.0 %copy-start = (bf16[1,64,8192]{2,1,0:T(8,128)(2,1)S(1)}, bf16[1,64,8192]{2,1,0:T(8,128)(2,1)}, u32[]{:S(2)}) copy-start(bf16[1,64,8192]{2,1,0:T(8,128)(2,1)} %all-gather.5.cloned.1.call-done) | copy-start | bytes 3145732
  88.9 6.7 %copy-start.1 = (bf16[1,64,8192]{2,1,0:T(8,128)(2,1)S(1)}, bf16[1,64,8192]{2,1,0:T(8,128)(2,1)}, u32[]{:S(2)}) copy-start(bf16[1,64,8192]{2,1,0:T(8,128)(2,1)} %all-gather.7.cloned.1.call-done) | copy-start | bytes 3145732
  134.9 271.5 %all-reduce.5.cloned.1.call-start = ((), (), s32[]{:S(2)}) async-start(), calls=%async_computation.2 | async-start | bytes 8388608 | tf_op jit(solution)/shard_map/psum | solution.py:28
  250.2 1.4 copy-start.3
  258.2 14.6 %copy-start.2 = (f32[64,8192]{1,0:T(8,128)S(1)}, f32[64,8192]{1,0:T(8,128)}, u32[]{:S(2)}) copy-start(f32[64,8192]{1,0:T(8,128)} %get-tuple-element.12) | copy-start | bytes 6291460
Sparse Core Ops, SparseCore 0:
  9.5 39.3 all-gather.4
  51.0 36.2 all-gather.6
  135.1 110.9 all-reduce.6
  296.0 110.3 all-reduce.4
where the time goes:
time: 416 us
  waiting for transfers between devices  298 us (72%)
  matrix products  90.2 us (22%)
  between operations  13.2 us (3%)
  other arithmetic  9.94 us (2%)
    psum x2, waiting for transfers between devices, body(): branch = lax.psum(partials, 'width')  221 us
    all_gather x2, waiting for transfers between devices, body(): lax.all_gather(stream_in[micro_index], 'width', axis=1, tiled=True)  75.8 us
    dot_general x4, matrix products, body(): jnp.dot(hidden, w_down[depth], preferred_element_type=jnp.float32)  63.7 us
    dot_general x4, matrix products, body(): jnp.dot(normed, w_gate[depth], preferred_element_type=jnp.float32)  26.5 us
  transfers between devices with their start and end apart: 4, of which 4 were waited for; matrix products, arithmetic and copies ran while one was open for 1% of the time, Pallas kernels for 0%

commit v1 on v0

--- a/solution.py
+++ b/solution.py
@@ -8,12 +8,17 @@
 
 
 def body(stream_in, norm_gain, w_gate, w_up, w_down):
+
+    def keep_up_strings(unit):
+        wide_n = lax.axis_size("width")
+        buffer = tuple((wide_n if ii == 1 else 1 for ii in range(unit.ndim)))
+        return lax.all_to_all(
+            jnp.tile(unit, buffer), "width", split_axis=1, concat_axis=1, tiled=True
+        )
+
     width_local = stream_in.shape[2]
     offset = lax.axis_index("width") * width_local
-    starts = [
-        lax.all_gather(stream_in[micro_index], "width", axis=1, tiled=True)
-        for micro_index in range(MICRO)
-    ]
+    starts = [keep_up_strings(stream_in[micro_index]) for micro_index in range(MICRO)]
     results = []
     for micro_index in range(MICRO):
         stream = starts[micro_index]

time: 416 us -> 403 us (0.969)
  waiting for transfers between devices: 298 us -> 244 us
  blocking collectives: 0 us -> 31.9 us
  starting transfers between devices: 0.3 us -> 5.11 us
    all_gather x2 -> x0, waiting for transfers between devices: 75.8 us -> none  [body(): lax.all_gather(stream_in[micro_index], 'width', axis=1, tiled=True)]
    all_to_all x0 -> x1, blocking collectives: none -> 31.9 us  [keep_up_strings(): lax.all_to_all(jnp.tile(unit, buffer), 'width', split_axis=1, concat_axis...]
    all_to_all x0 -> x1, waiting for transfers between devices: none -> 22.4 us  [keep_up_strings(): lax.all_to_all(jnp.tile(unit, buffer), 'width', split_axis=1, concat_axis...]
    all_to_all x0 -> x1, starting transfers between devices: none -> 5.02 us  [keep_up_strings(): lax.all_to_all(jnp.tile(unit, buffer), 'width', split_axis=1, concat_axis...]
  transfers between devices with their start and end apart: 4 -> 3, of which waited for: 4 -> 3; matrix products, arithmetic and copies ran while one was open for 1% -> 1% of each run, Pallas kernels for 0% -> 0%
where the time goes in v1:
time: 403 us; the launch traced here: 402 us
  waiting for transfers between devices  244 us (61%)
  matrix products  93 us (23%)
  blocking collectives  31.9 us (8%)
  between operations  13.6 us (3%)
  other arithmetic  9.25 us (2%)
  local copies, waits for them, and re-layouts  5.48 us (1%)
  starting transfers between devices  5.11 us (1%)
    psum x2, waiting for transfers between devices, body(): branch = lax.psum(partials, 'width')  221 us
    dot_general x4, matrix products, body(): jnp.dot(hidden, w_down[depth], preferred_element_type=jnp.float32)  63.6 us
    all_to_all x1, blocking collectives, keep_up_strings(): lax.all_to_all(jnp.tile(unit, buffer), 'width', split_axis=1, concat_axis...  31.9 us
    dot_general x4, matrix products, body(): jnp.dot(normed, w_gate[depth], preferred_element_type=jnp.float32)  29.4 us
    all_to_all x1, waiting for transfers between devices, keep_up_strings(): lax.all_to_all(jnp.tile(unit, buffer), 'width', split_axis=1, concat_axis...  22.4 us
  transfers between devices with their start and end apart: 3, of which 3 were waited for; matrix products, arithmetic and copies ran while one was open for 1% of the time, Pallas kernels for 0%

profile of v1, /device:TPU:0, one launch (start us, length us, event | category | flops | bytes accessed | tf_op | source)
XLA Modules:
  0.0 402.3 jit_solution(13399095424059408358)
XLA Ops:
  6.5 0.9 slice_bitcast_fusion.1
  7.4 0.1 tile.19
  7.5 31.9 %all_to_all.12 = bf16[64,16,512]{2,0,1:T(8,128)(2,1)S(1)} all-to-all(bf16[64,16,512]{2,0,1:T(8,128)(2,1)S(1)} %tile.19), channel_id=1, replica_groups=mesh['groups'=2,'width'=16] {'width'}, dimensions={1} | all-to-all | bytes 2097152 | tf_op jit(solution)/shard_map/all_to_all | solution.py:15
  39.4 0.0 copy-start.3
  39.4 1.1 tile.17
  40.5 5.0 %all-to-all-start = ((bf16[64,16,512]{2,0,1:T(8,128)(2,1)}), bf16[64,16,512]{2,0,1:T(8,128)(2,1)S(1)}, u32[]{:S(2)}, u32[]{:S(2)}) async-start(bf16[64,16,512]{2,0,1:T(8,128)(2,1)} %tile.17), calls=%async_computation | async-start | bytes 2097152 | tf_op jit(solution)/shard_map/all_to_all | solution.py:15
  45.5 0.0 all-reduce.7.cloned.1.call-start
  45.6 0.0 copy-done.3
  45.6 0.1 fusion.112
  45.7 0.3 fusion.39
  46.0 22.4 %all-to-all-done = bf16[64,16,512]{2,0,1:T(8,128)(2,1)S(1)} async-done(((bf16[64,16,512]{2,0,1:T(8,128)(2,1)}), bf16[64,16,512]{2,0,1:T(8,128)(2,1)S(1)}, u32[]{:S(2)}, u32[]{:S(2)}) %all-to-all-start) | async-done | bytes 1048608 | tf_op jit(solution)/shard_map/all_to_all | solution.py:15
  68.4 0.3 fusion.36
  68.8 0.7 fusion.69
  69.4 0.1 copy.13
  69.5 0.1 copy.15
  69.6 0.0 copy-start.2
  69.6 8.6 %fusion.22 = f32[64,896]{1,0:T(8,128)} fusion(bf16[64,8192]{1,0:T(8,128)(2,1)S(1)} %bitcast.81, bf16[2,8192,896]{2,1,0:T(8,128)(2,1)} %param.7), kind=kOutput, calls=%fused_computation.22 | convolution fusion | flops 939524096 | bytes 15958016 | tf_op jit(solution)/shard_map/dot_general | solution.py:29
  78.3 0.0 copy-done.2
  78.3 7.6 %fusion.20 = f32[64,896]{1,0:T(8,128)S(1)} fusion(bf16[64,8192]{1,0:T(8,128)(2,1)S(1)} %bitcast.83, bf16[2,8192,896]{2,1,0:T(8,128)(2,1)} %param.7), kind=kOutput, calls=%fused_computation.20 | convolution fusion | flops 939524096 | bytes 15958016 | tf_op jit(solution)/shard_map/dot_general | solution.py:29
  85.9 16.1 %fusion.14 = f32[64,8192]{1,0:T(8,128)} fusion(bf16[2,896,8192]{2,1,0:T(8,128)(2,1)} %param.9, bf16[64,8192]{1,0:T(8,128)(2,1)S(1)} %bitcast.82, bf16[2,8192,896]{2,1,0:T(8,128)(2,1)} %param.8, f32[64,896]{1,0:T(8,128)} %fusion.22), kind=kOutput, calls=%fused_computation.14 | convolution fusion | flops 1879392256 | bytes 32735232 | tf_op jit(solution)/shard_map/dot_general | solution.py:32
  102.0 16.5 %fusion.12 = f32[64,8192]{1,0:T(8,128)} fusion(bf16[2,896,8192]{2,1,0:T(8,128)(2,1)} %param.9, bf16[64,8192]{1,0:T(8,128)(2,1)} %bitcast.84, bf16[2,8192,896]{2,1,0:T(8,128)(2,1)} %param.8, f32[64,896]{1,0:T(8,128)S(1)} %fusion.20), kind=kOutput, calls=%fused_computation.12 | convolution fusion | flops 1879392256 | bytes 32735232 | tf_op jit(solution)/shard_map/dot_general | solution.py:32
  118.5 0.0 all-reduce.7.cloned.1.call-update
  118.5 0.0 all-reduce.5.cloned.1.call-start
  118.5 0.3 convert_bitcast_fusion.1
  118.8 0.2 copy.12
  119.0 0.3 convert_bitcast_fusion
  119.3 1.6 copy.14
  120.9 111.1 %all-reduce.7.cloned.1.call-done = (f32[64,8192]{1,0:T(8,128)}, f32[64,8192]{1,0:T(8,128)}) async-done(((f32[64,8192]{1,0:T(8,128)}, f32[64,8192]{1,0:T(8,128)}), (f32[64,8192]{1,0:T(8,128)}, f32[64,8192]{1,0:T(8,128)})) %all-reduce.7.cloned.1.call-update) | async-done | bytes 4194320 | tf_op jit(solution)/shard_map/psum | solution.py:33
  232.0 4.8 %multiply_reduce_fusion = (f32[64]{0:T(128)S(1)}, f32[64,8192]{1,0:T(8,128)}, f32[64]{0:T(128)S(1)}, f32[64,8192]{1,0:T(8,128)S(1)}) fusion(f32[64,8192]{1,0:T(8,128)} %bitcast.80, f32[64,8192]{1,0:T(8,128)} %get-tuple-element.7, f32[64,8192]{1,0:T(8,128)S(1)} %bitcast.79, f32[64,8192]{1,0:T(8,128)} %get-tuple-element.8), kind=kLoop, calls=%fused_computation.49 | loop fusion | flops 5242752 | bytes 12583424 | tf_op jit(solution)/shard_map/reduce_sum | solution.py:27
  236.8 0.0 copy-start.1
  236.8 1.3 copy-done.1
  238.1 6.6 %fusion.10 = f32[64,896]{1,0:T(8,128)S(1)} fusion(bf16[2,8192,896]{2,1,0:T(8,128)(2,1)} %param.7, f32[64,8192]{1,0:T(8,128)S(1)} %get-tuple-element.20, f32[8192]{0:T(1024)S(1)} %bitcast.85, f32[64]{0:T(128)S(1)} %add_rsqrt_fusion.2), kind=kOutput, calls=%fused_computation.10 | convolution fusion | flops 941096960 | bytes 17039616 | tf_op jit(solution)/shard_map/dot_general | solution.py:29
  244.8 0.0 copy-start
  244.8 14.6 %fusion.2 = f32[64,8192]{1,0:T(8,128)} fusion(bf16[2,896,8192]{2,1,0:T(8,128)(2,1)} %param.9, bf16[2,8192,896]{2,1,0:T(8,128)(2,1)} %param.8, f32[64,896]{1,0:T(8,128)S(1)} %fusion.10, f32[64,8192]{1,0:T(8,128)} %copy-done.1, f32[8192]{0:T(1024)S(1)} %bitcast.86, f32[64]{0:T(128)S(1)} %add_rsqrt_fusion.2), kind=kOutput, calls=%fused_computation.2 | convolution fusion | flops 1880965120 | bytes 33816832 | tf_op jit(solution)/shard_map/dot_general | solution.py:32
  259.4 0.0 copy-done
  259.4 6.6 %fusion.8 = f32[64,896]{1,0:T(8,128)S(1)} fusion(bf16[2,8192,896]{2,1,0:T(8,128)(2,1)} %param.7, f32[64,8192]{1,0:T(8,128)S(1)} %copy-done, f32[64]{0:T(128)S(1)} %add_rsqrt_fusion, f32[8192]{0:T(1024)S(1)} %bitcast.87), kind=kOutput, calls=%fused_computation.8 | convolution fusion | flops 941096960 | bytes 17039616 | tf_op jit(solution)/shard_map/dot_general | solution.py:29
  266.0 16.4 %fusion = f32[64,8192]{1,0:T(8,128)} fusion(bf16[2,896,8192]{2,1,0:T(8,128)(2,1)} %param.9, bf16[2,8192,896]{2,1,0:T(8,128)(2,1)} %param.8, f32[64,896]{1,0:T(8,128)S(1)} %fusion.8, f32[64,8192]{1,0:T(8,128)S(1)} %copy-done, f32[64]{0:T(128)S(1)} %add_rsqrt_fusion, f32[8192]{0:T(1024)S(1)} %bitcast.88), kind=kOutput, calls=%fused_computation | convolution fusion | flops 1880965120 | bytes 33816832 | tf_op jit(solution)/shard_map/dot_general | solution.py:32
  282.4 0.0 all-reduce.5.cloned.1.call-update
  282.4 110.4 %all-reduce.5.cloned.1.call-done = (f32[64,8192]{1,0:T(8,128)}, f32[64,8192]{1,0:T(8,128)}) async-done(((f32[64,8192]{1,0:T(8,128)}, f32[64,8192]{1,0:T(8,128)}), (f32[64,8192]{1,0:T(8,128)}, f32[64,8192]{1,0:T(8,128)})) %all-reduce.5.cloned.1.call-update) | async-done | bytes 4194320 | tf_op jit(solution)/shard_map/psum | solution.py:33
  392.8 1.0 fusion.104
  393.8 0.9 fusion.105
  394.7 0.7 pad_maximum_fusion
  (5 shorter events, 0.0 us)
Async XLA Ops:
  39.4 6.2 %copy-start.3 = (f32[2,8192]{1,0:T(2,128)S(1)}, f32[2,8192]{1,0:T(2,128)}, u32[]{:S(2)}) copy-start(f32[2,8192]{1,0:T(2,128)} %param.6) | copy-start | bytes 196612
  40.5 27.9 %all-to-all-start = ((bf16[64,16,512]{2,0,1:T(8,128)(2,1)}), bf16[64,16,512]{2,0,1:T(8,128)(2,1)S(1)}, u32[]{:S(2)}, u32[]{:S(2)}) async-start(bf16[64,16,512]{2,0,1:T(8,128)(2,1)} %tile.17), calls=%async_computation | async-start | bytes 2097152 | tf_op jit(solution)/shard_map/all_to_all | solution.py:15
  45.5 186.4 %all-reduce.7.cloned.1.call-start = ((), (), s32[]{:S(2)}) async-start(), calls=%async_computation.3 | async-start | bytes 8388608 | tf_op jit(solution)/shard_map/psum | solution.py:33
  69.6 8.7 %copy-start.2 = (bf16[16,8,8,512]{3,2,0,1:T(8,128)(2,1)}, bf16[16,8,8,512]{3,2,0,1:T(8,128)(2,1)S(1)}, u32[]{:S(2)}) copy-start(bf16[16,8,8,512]{3,2,0,1:T(8,128)(2,1)S(1)} %copy.15) | copy-start | bytes 3145732
  118.5 274.3 %all-reduce.5.cloned.1.call-start = ((), (), s32[]{:S(2)}) async-start(), calls=%async_computation.2 | async-start | bytes 8388608 | tf_op jit(solution)/shard_map/psum | solution.py:33
  236.8 1.4 copy-start.1
  244.8 14.6 %copy-start = (f32[64,8192]{1,0:T(8,128)S(1)}, f32[64,8192]{1,0:T(8,128)}, u32[]{:S(2)}) copy-start(f32[64,8192]{1,0:T(8,128)} %get-tuple-element.12) | copy-start | bytes 6291460
Sparse Core Ops, SparseCore 0:
  118.6 113.3 all-reduce.6
  282.5 110.2 all-reduce.4
